TPU v7x, 32 devices: a whole 2x2x4 slice. The times are simulated.
32 devices in a mesh: dp: 8 (over y, x, core), tensor: 4 (over z).
Axes of the slice: x: 2, y: 2, z: 4, core: 2. Of those that a mesh axis runs over, the one named last changes fastest.
Arguments:
- inputs: bfloat16 [16, 1024, 1024], P('dp', 'tensor'), may hold values from -6 to 6
- cotangent: bfloat16 [16, 1024, 1024], P('dp', 'tensor'), may hold values from -6 to 6
- lengths: int32 [16], P('dp'), may hold values from 1 to 1024, as said below
- block_ids: int32 [16, 1024], P('dp'), may hold values from 0 to 7, never falling along the last dimension, each value on 1 to 256 neighbouring positions
- ln1_gain: float32 [1024], replicated, may hold values from 0.5 to 1.5
- ln1_bias: float32 [1024], replicated, may hold values from -1 to 1
- ln2_gain: float32 [1024], replicated, may hold values from 0.5 to 1.5
- ln2_bias: float32 [1024], replicated, may hold values from -1 to 1
- w_qkv: bfloat16 [1024, 3072], P('dp', 'tensor'), may hold values from -0.1875 to 0.1875
- b_qkv: float32 [3072], P('tensor'), may hold values from -1 to 1
- w_out: bfloat16 [1024, 1024], P('dp', 'tensor'), may hold values from -1 to 1
- b_out: float32 [1024], replicated, may hold values from -1 to 1
- w_up: bfloat16 [1024, 4096], P('dp', 'tensor'), may hold values from -0.1875 to 0.1875
- b_up: float32 [4096], P('tensor'), may hold values from -1 to 1
- w_down: bfloat16 [1024, 4096], P('dp', 'tensor'), may hold values from -0.09375 to 0.09375
- b_down: float32 [1024], replicated, may hold values from -1 to 1
Outputs:
- layer_out: bfloat16 [16, 1024, 1024], P('dp', 'tensor')
- grad_inputs: float32 [16, 1024, 1024], P('dp', 'tensor')
- grad_w_qkv: float32 [1024, 3072], P('dp', 'tensor')
- grad_w_out: float32 [1024, 1024], P('dp', 'tensor')
- grad_w_up: float32 [1024, 4096], P('dp', 'tensor')
- grad_w_down: float32 [1024, 4096], P('dp', 'tensor')
- grad_b_qkv: float32 [3072], P('tensor')
- grad_b_up: float32 [4096], P('tensor')
- grad_ln1_gain: float32 [1024], replicated
- grad_ln1_bias: float32 [1024], replicated
- grad_ln2_gain: float32 [1024], replicated
- grad_ln2_bias: float32 [1024], replicated
- grad_b_out: float32 [1024], replicated
- grad_b_down: float32 [1024], replicated
Inputs may be any that keep to these rules, and one draw needn't show every extreme that they name: `lengths`: live tokens of each sequence, at its start; keys from the length on are padding; some sequence has all 1024 live. `block_ids`: along each sequence the block number starts at 0 and never falls; each block spans 1 to 256 consecutive positions and some block spans exactly 256.
All inputs are finite; a program needn't handle non-finite values.
Results may differ from a plain program's by a relative error of at most 0.0098.
Values may be sent and summed in bfloat16 or wider, within the bound.
A program may use at most 256 MiB of HBM per device.

v0:
```python
import jax
import jax.numpy as jnp
from jax import lax
from jax.sharding import PartitionSpec as P

HEAD = 64
ROT = 16
BLOCK = 256
MICRO = 2


def layer_norm(values, ln_gain, ln_bias):
    centre = jnp.mean(values, axis=-1, keepdims=True)
    shifted = values - centre
    spread = jnp.mean(shifted * shifted, axis=-1, keepdims=True)
    return shifted * lax.rsqrt(spread + 1e-05) * ln_gain + ln_bias


def rope_tables(length, rotary):
    halved = rotary // 2
    frequency = 1.0 / 10000.0 ** (jnp.arange(halved, dtype=jnp.float32) * (2.0 / rotary))
    angles = jnp.arange(length, dtype=jnp.float32)[:, None] * frequency[None, :]
    angles = jnp.concatenate([angles, angles], axis=1)[:, None, :]
    return (jnp.cos(angles), jnp.sin(angles))


def rotate(head_rows, cos_table, sin_table, rotary):
    halved = rotary // 2
    moving = head_rows[..., :rotary]
    turned = jnp.concatenate([-moving[..., halved:], moving[..., :halved]], axis=-1)
    moving = moving * cos_table + turned * sin_table
    return jnp.concatenate([moving, head_rows[..., rotary:]], axis=-1)


def visible(block_rows, limits, first_row, tile_rows, key_end):
    own_ids = block_rows[:, first_row : first_row + tile_rows]
    key_pos = jnp.arange(key_end, dtype=jnp.int32)
    allowed = (block_rows[:, None, :key_end] <= own_ids[:, :, None]) & (
        key_pos[None, None, :] < limits[:, None, None]
    )
    return allowed[:, None]


def gelu_exact(argument):
    return jax.nn.gelu(argument, approximate=False)


def on_device(
    inputs,
    cotangent,
    lengths,
    block_ids,
    ln1_gain,
    ln1_bias,
    ln2_gain,
    ln2_bias,
    w_qkv,
    b_qkv,
    w_out,
    b_out,
    w_up,
    b_up,
    w_down,
    b_down,
):
    model_width = inputs.shape[2]
    per_micro = inputs.shape[0] // MICRO
    length = block_ids.shape[1]
    tile_rows = min(512, length)
    heads_here = w_qkv.shape[1] // (3 * HEAD)
    scaling = HEAD ** (-0.5)
    cos_table, sin_table = rope_tables(length, ROT)
    grad_qkv = jnp.zeros((model_width, w_qkv.shape[1]), jnp.float32)
    grad_outw = jnp.zeros((model_width, w_out.shape[1]), jnp.float32)
    grad_upw = jnp.zeros((model_width, w_up.shape[1]), jnp.float32)
    grad_downw = jnp.zeros((model_width, w_down.shape[1]), jnp.float32)
    sum_bias_qkv = jnp.zeros((w_qkv.shape[1],), jnp.float32)
    sum_bias_up = jnp.zeros((w_up.shape[1],), jnp.float32)
    sum_gain_one = jnp.zeros((model_width,), jnp.float32)
    sum_bias_one = jnp.zeros((model_width,), jnp.float32)
    sum_gain_two = jnp.zeros((model_width,), jnp.float32)
    sum_bias_two = jnp.zeros((model_width,), jnp.float32)
    sum_slope = jnp.zeros((model_width,), jnp.float32)
    out_rows = []
    grad_rows = []
    tile_starts = list(range(0, length, tile_rows))
    key_ends = [min(length, first_row + tile_rows + BLOCK) for first_row in tile_starts]
    for micro_idx in range(MICRO):
        first_seq = micro_idx * per_micro
        last_seq = first_seq + per_micro
        residual = inputs[first_seq:last_seq].astype(jnp.float32)
        limits = lengths[first_seq:last_seq]
        block_rows = block_ids[first_seq:last_seq]
        value_one, norm_one_back = jax.vjp(layer_norm, residual, ln1_gain, ln1_bias)
        value_two, norm_two_back = jax.vjp(layer_norm, residual, ln2_gain, ln2_bias)
        whole_one, whole_two = (
            lax.all_gather(value_one.astype(jnp.bfloat16), "tensor", axis=1, tiled=True),
            lax.all_gather(value_two.astype(jnp.bfloat16), "tensor", axis=1, tiled=True),
        )
        qkv_full, out_full, up_full, down_full = (
            lax.all_gather(w_qkv, "dp", axis=0, tiled=True),
            lax.all_gather(w_out, "dp", axis=0, tiled=True),
            lax.all_gather(w_up, "dp", axis=0, tiled=True),
            lax.all_gather(w_down, "dp", axis=0, tiled=True),
        )
        projected = (
            jnp.einsum("bsd,dc->bsc", whole_one, qkv_full, preferred_element_type=jnp.float32)
            + b_qkv
        )
        projected = projected.reshape(per_micro, length, heads_here, 3, HEAD)
        queries = rotate(projected[:, :, :, 0], cos_table, sin_table, ROT).astype(jnp.bfloat16)
        key_rows = rotate(projected[:, :, :, 1], cos_table, sin_table, ROT).astype(jnp.bfloat16)
        values = projected[:, :, :, 2].astype(jnp.bfloat16)
        scaled_q = (queries * jnp.bfloat16(scaling)).transpose(0, 2, 1, 3)
        keys_hd = key_rows.transpose(0, 2, 1, 3)
        values_hd = values.transpose(0, 2, 1, 3)
        log_sums = []
        mixed_parts = []
        for first_row, key_end in zip(tile_starts, key_ends):
            q_block = scaled_q[:, :, first_row : first_row + tile_rows]
            allowed = visible(block_rows, limits, first_row, tile_rows, key_end)
            scores = jnp.einsum(
                "bhqe,bhke->bhqk",
                q_block,
                keys_hd[:, :, :key_end],
                preferred_element_type=jnp.float32,
            )
            scores = jnp.where(allowed, scores, -1e30)
            row_peak = jnp.max(scores, axis=-1)
            powered = jnp.exp(scores - row_peak[..., None])
            totals = jnp.sum(powered, axis=-1)
            soft_low = (powered / totals[..., None]).astype(jnp.bfloat16)
            log_sums.append(row_peak + jnp.log(totals))
            mixed_parts.append(
                jnp.einsum(
                    "bhqk,bhke->bhqe",
                    soft_low,
                    values_hd[:, :, :key_end],
                    preferred_element_type=jnp.float32,
                )
            )
        attended = (
            jnp.concatenate(mixed_parts, axis=2)
            .transpose(0, 2, 1, 3)
            .reshape(per_micro, length, heads_here * HEAD)
            .astype(jnp.bfloat16)
        )
        partial_sum = jnp.einsum(
            "bsf,df->bsd", attended, out_full, preferred_element_type=jnp.float32
        )
        hidden_pre = (
            jnp.einsum("bsd,df->bsf", whole_two, up_full, preferred_element_type=jnp.float32) + b_up
        )
        gelu_value, gelu_back = jax.vjp(gelu_exact, hidden_pre)
        activated = gelu_value.astype(jnp.bfloat16)
        partial_sum = partial_sum + jnp.einsum(
            "bsf,df->bsd", activated, down_full, preferred_element_type=jnp.float32
        )
        reduced = lax.psum_scatter(partial_sum, "tensor", scatter_dimension=1, tiled=True)
        out_rows.append((residual + reduced + b_out + b_down).astype(jnp.bfloat16))
        slope_local = cotangent[first_seq:last_seq]
        slope = lax.all_gather(slope_local, "tensor", axis=1, tiled=True)
        qkv_full, out_full, up_full, down_full = (
            lax.all_gather(w_qkv, "dp", axis=0, tiled=True),
            lax.all_gather(w_out, "dp", axis=0, tiled=True),
            lax.all_gather(w_up, "dp", axis=0, tiled=True),
            lax.all_gather(w_down, "dp", axis=0, tiled=True),
        )
        grad_outw = grad_outw + jnp.einsum(
            "bsd,bsf->df", slope, attended, preferred_element_type=jnp.float32
        )
        grad_downw = grad_downw + jnp.einsum(
            "bsd,bsf->df", slope, activated, preferred_element_type=jnp.float32
        )
        grad_att = jnp.einsum(
            "bsd,df->bsf", slope, out_full, preferred_element_type=jnp.float32
        ).astype(jnp.bfloat16)
        grad_att = grad_att.reshape(per_micro, length, heads_here, HEAD).transpose(0, 2, 1, 3)
        grad_act = jnp.einsum("bsd,df->bsf", slope, down_full, preferred_element_type=jnp.float32)
        grad_hidden = gelu_back(grad_act)[0].astype(jnp.bfloat16)
        grad_upw = grad_upw + jnp.einsum(
            "bsd,bsf->df", whole_two, grad_hidden, preferred_element_type=jnp.float32
        )
        sum_bias_up = sum_bias_up + jnp.sum(grad_hidden.astype(jnp.float32), axis=(0, 1))
        grad_two = jnp.einsum(
            "bsf,df->bsd", grad_hidden, up_full, preferred_element_type=jnp.float32
        )
        grad_keys = jnp.zeros((per_micro, heads_here, length, HEAD), jnp.float32)
        grad_values = jnp.zeros((per_micro, heads_here, length, HEAD), jnp.float32)
        query_parts = []
        for index_tile, first_row in enumerate(tile_starts):
            key_end = key_ends[index_tile]
            q_block = scaled_q[:, :, first_row : first_row + tile_rows]
            g_block = grad_att[:, :, first_row : first_row + tile_rows]
            k_block = keys_hd[:, :, :key_end]
            allowed = visible(block_rows, limits, first_row, tile_rows, key_end)
            scores = jnp.einsum(
                "bhqe,bhke->bhqk", q_block, k_block, preferred_element_type=jnp.float32
            )
            scores = jnp.where(allowed, scores, -1e30)
            soft_full = jnp.exp(scores - log_sums[index_tile][..., None])
            soft_low = soft_full.astype(jnp.bfloat16)
            value_part = jnp.einsum(
                "bhqk,bhqe->bhke", soft_low, g_block, preferred_element_type=jnp.float32
            )
            grad_values = grad_values.at[:, :, :key_end].add(value_part)
            grad_soft = jnp.einsum(
                "bhqe,bhke->bhqk",
                g_block,
                values_hd[:, :, :key_end],
                preferred_element_type=jnp.float32,
            )
            centred = jnp.sum(soft_full * grad_soft, axis=-1)
            grad_scores = (soft_full * (grad_soft - centred[..., None])).astype(jnp.bfloat16)
            query_parts.append(
                jnp.einsum(
                    "bhqk,bhke->bhqe", grad_scores, k_block, preferred_element_type=jnp.float32
                )
                * scaling
            )
            key_part = jnp.einsum(
                "bhqk,bhqe->bhke", grad_scores, q_block, preferred_element_type=jnp.float32
            )
            grad_keys = grad_keys.at[:, :, :key_end].add(key_part)
        grad_queries = jnp.concatenate(query_parts, axis=2).transpose(0, 2, 1, 3)
        grad_keys = grad_keys.transpose(0, 2, 1, 3)
        grad_values = grad_values.transpose(0, 2, 1, 3)
        grad_projected = jnp.stack(
            [
                rotate(grad_queries, cos_table, -sin_table, ROT),
                rotate(grad_keys, cos_table, -sin_table, ROT),
                grad_values,
            ],
            axis=3,
        )
        grad_projected = grad_projected.reshape(per_micro, length, 3 * heads_here * HEAD).astype(
            jnp.bfloat16
        )
        grad_qkv = grad_qkv + jnp.einsum(
            "bsd,bsc->dc", whole_one, grad_projected, preferred_element_type=jnp.float32
        )
        sum_bias_qkv = sum_bias_qkv + jnp.sum(grad_projected.astype(jnp.float32), axis=(0, 1))
        grad_one = jnp.einsum(
            "bsc,dc->bsd", grad_projected, qkv_full, preferred_element_type=jnp.float32
        )
        slope_rows = slope_local.astype(jnp.float32)
        back_one, back_two = (
            lax.psum_scatter(grad_one, "tensor", scatter_dimension=1, tiled=True),
            lax.psum_scatter(grad_two, "tensor", scatter_dimension=1, tiled=True),
        )
        input_one, gain_one, bias_one = norm_one_back(back_one)
        input_two, gain_two, bias_two = norm_two_back(back_two)
        grad_rows.append(slope_rows + input_one + input_two)
        sum_gain_one = sum_gain_one + gain_one
        sum_bias_one = sum_bias_one + bias_one
        sum_gain_two = sum_gain_two + gain_two
        sum_bias_two = sum_bias_two + bias_two
        sum_slope = sum_slope + jnp.sum(slope_rows, axis=(0, 1))
    reduced_grads = (
        lax.psum_scatter(grad_qkv, "dp", scatter_dimension=0, tiled=True),
        lax.psum_scatter(grad_outw, "dp", scatter_dimension=0, tiled=True),
        lax.psum_scatter(grad_upw, "dp", scatter_dimension=0, tiled=True),
        lax.psum_scatter(grad_downw, "dp", scatter_dimension=0, tiled=True),
    )
    bias_qkv_total, bias_up_total = lax.psum((sum_bias_qkv, sum_bias_up), "dp")
    shared = lax.psum(
        (sum_gain_one, sum_bias_one, sum_gain_two, sum_bias_two, sum_slope), ("dp", "tensor")
    )
    return (
        jnp.concatenate(out_rows, axis=0),
        jnp.concatenate(grad_rows, axis=0),
        reduced_grads[0],
        reduced_grads[1],
        reduced_grads[2],
        reduced_grads[3],
        bias_qkv_total,
        bias_up_total,
        shared[0],
        shared[1],
        shared[2],
        shared[3],
        shared[4],
        shared[4],
    )


def solution(mesh):
    in_specs = (
        P("dp", "tensor", None),
        P("dp", "tensor", None),
        P("dp"),
        P("dp", None),
        P(),
        P(),
        P(),
        P(),
        P("dp", "tensor"),
        P("tensor"),
        P("dp", "tensor"),
        P(),
        P("dp", "tensor"),
        P("tensor"),
        P("dp", "tensor"),
        P(),
    )
    out_specs = (
        P("dp", "tensor", None),
        P("dp", "tensor", None),
        P("dp", "tensor"),
        P("dp", "tensor"),
        P("dp", "tensor"),
        P("dp", "tensor"),
        P("tensor"),
        P("tensor"),
        P(),
        P(),
        P(),
        P(),
        P(),
        P(),
    )
    return jax.shard_map(
        on_device, mesh=mesh, in_specs=in_specs, out_specs=out_specs, check_vma=False
    )
```

profile of v0, /device:TPU:0, one launch (start us, length us, event | category | flops | bytes accessed | tf_op | source)
XLA Modules:
  0.0 1063.5 jit_solution(9621609152329100266)
XLA Ops:
  11.7 3.2 fusion.173
  24.5 12.7 %all_gather.44 = bf16[1024,256]{1,0:T(8,128)(2,1)S(1)} all-gather(bf16[128,256]{1,0:T(8,128)(2,1)S(1)} %copy-done.88), channel_id=1, replica_groups=mesh['dp'=8,'tensor'=4] {'dp'}, dimensions={0}, use_global_device_ids=true | all-gather | bytes 589824 | tf_op jit(solution)/shard_map/all_gather | solution.py:102
  39.7 48.1 %all-gather.10.cloned.1.call-done = bf16[1,1024,1024]{2,1,0:T(8,128)(2,1)} async-done(((bf16[1,256,1024]{2,1,0:T(8,128)(2,1)}), bf16[1,1024,1024]{2,1,0:T(8,128)(2,1)}) %all-gather.10.cloned.1.call-update) | async-done | bytes 2097168 | tf_op jit(solution)/shard_map/all_gather | solution.py:97
  87.8 3.9 fusion.85
  96.9 37.2 %all-gather.20.cloned.1.call-done = bf16[1,1024,1024]{2,1,0:T(8,128)(2,1)} async-done(((bf16[1,256,1024]{2,1,0:T(8,128)(2,1)}), bf16[1,1024,1024]{2,1,0:T(8,128)(2,1)}) %all-gather.20.cloned.1.call-update) | async-done | bytes 2097168 | tf_op jit(solution)/shard_map/all_gather | solution.py:97
  134.1 3.9 fusion.91
  147.8 2.8 fusion.161
  150.5 29.7 %all-gather.24.cloned.1.call-done = bf16[1,1024,1024]{2,1,0:T(8,128)(2,1)} async-done(((bf16[1,256,1024]{2,1,0:T(8,128)(2,1)}), bf16[1,1024,1024]{2,1,0:T(8,128)(2,1)}) %all-gather.24.cloned.1.call-update) | async-done | bytes 2097168 | tf_op jit(solution)/shard_map/all_gather | solution.py:162
  182.6 4.8 multiply_reduce_fusion.3
  197.7 3.6 fusion.155
  212.0 3.8 fusion.154
  215.9 10.4 all-gather.26.cloned.1.call-done
  226.3 3.3 fusion.145
  234.4 6.3 multiply_reduce_fusion.1
  251.7 21.3 %all-gather.22.cloned.1.call-done = bf16[1,1024,1024]{2,1,0:T(8,128)(2,1)} async-done(((bf16[1,256,1024]{2,1,0:T(8,128)(2,1)}), bf16[1,1024,1024]{2,1,0:T(8,128)(2,1)}) %all-gather.22.cloned.1.call-update) | async-done | bytes 2097168 | tf_op jit(solution)/shard_map/all_gather | solution.py:98
  273.0 28.5 %all-gather.16.cloned.1.call-done = bf16[1024,1024]{1,0:T(8,128)(2,1)} async-done(((bf16[128,1024]{1,0:T(8,128)(2,1)}), bf16[1024,1024]{1,0:T(8,128)(2,1)}) %all-gather.16.cloned.1.call-update) | async-done | bytes 2097168 | tf_op jit(solution)/shard_map/all_gather | solution.py:103
  301.5 6.6 fusion.66
  308.2 41.5 %all-gather.14.cloned.1.call-done = bf16[1,1024,1024]{2,1,0:T(8,128)(2,1)} async-done(((bf16[1,256,1024]{2,1,0:T(8,128)(2,1)}), bf16[1,1024,1024]{2,1,0:T(8,128)(2,1)}) %all-gather.14.cloned.1.call-update) | async-done | bytes 2097168 | tf_op jit(solution)/shard_map/all_gather | solution.py:98
  349.6 23.9 %multiply_convert_fusion.5 = (bf16[1024,1024]{1,0:T(8,128)(2,1)S(1)}, f32[1024,1024]{1,0:T(8,128)}, bf16[1024,1024]{1,0:T(8,128)(2,1)S(1)}, f32[1024,1024]{1,0:T(8,128)}, f32[1024,1024]{1,0:T(8,128)}) fusion(f32[1024]{0:T(1024)} %param.53, f32[1024,1024]{1,0:T(8,128)} %fusion.66, bf16[1024,1024]{1,0:T(8,128)(2,1)} %all-gather.16.cloned.1.call-done, ...), kind=kOutput, calls=%fused_computation.58 | convolution fusion | flops 2285895680 | bytes 25169920 | tf_op jit(solution)/shard_map/bsd,df->bsf/dot_general | solution.py:152
  376.7 4.5 add_bitcast_fusion
  385.4 3.0 fusion.156
  388.4 6.6 multiply_reduce_fusion
  409.1 3.9 convolution_bitcast_fusion.1
  414.7 4.4 fusion.151
  419.1 4.7 fusion.133
  425.5 3.9 convolution_bitcast_fusion
  431.1 7.4 convert_reduce_fusion
  439.9 4.4 convolution_bitcast_fusion.2
  445.9 6.8 convert_reduce_fusion.1
  454.2 4.5 convolution_bitcast_fusion.3
  460.2 4.0 fusion.252
  467.0 4.1 fusion.251
  471.1 2.8 add_bitcast_fusion.2
  475.3 3.6 fusion.68
  478.9 3.6 fusion.88
  482.6 4.8 fusion.64
  487.4 4.5 fusion.80
  492.2 16.0 %all-reduce.5 = (f32[768]{0:T(1024)}, f32[1024]{0:T(1024)}) all-reduce(f32[768]{0:T(1024)S(1)} %add.401, f32[1024]{0:T(1024)S(1)} %add.402), channel_id=1, replica_groups=mesh['dp'=8,'tensor'=4] {'dp'}, use_global_device_ids=true, to_apply=%region_36.37 | all-reduce | flops 1792 | bytes 14336 | tf_op jit(solution)/shard_map/psum | solution.py:265
  511.8 39.2 %reduce-scatter.15.cloned.1.call-done = f32[1,256,1024]{2,1,0:T(8,128)} async-done(((f32[1,1024,1024]{2,1,0:T(8,128)}), f32[1,256,1024]{2,1,0:T(8,128)}) %reduce-scatter.15.cloned.1.call-update) | async-done | bytes 1048592 | tf_op jit(solution)/shard_map/reduce_scatter | solution.py:248
  551.1 79.6 %reduce-scatter.19.cloned.1.call-done = f32[1,256,1024]{2,1,0:T(8,128)} async-done(((f32[1,1024,1024]{2,1,0:T(8,128)}), f32[1,256,1024]{2,1,0:T(8,128)}) %reduce-scatter.19.cloned.1.call-update) | async-done | bytes 1048592 | tf_op jit(solution)/shard_map/reduce_scatter | solution.py:248
  632.7 77.5 %reduce-scatter.21.cloned.1.call-done = f32[1,256,1024]{2,1,0:T(8,128)} async-done(((f32[1,1024,1024]{2,1,0:T(8,128)}), f32[1,256,1024]{2,1,0:T(8,128)}) %reduce-scatter.21.cloned.1.call-update) | async-done | bytes 1048592 | tf_op jit(solution)/shard_map/reduce_scatter | solution.py:249
  710.2 79.4 %reduce-scatter.17.cloned.1.call-done = f32[1,256,1024]{2,1,0:T(8,128)} async-done(((f32[1,1024,1024]{2,1,0:T(8,128)}), f32[1,256,1024]{2,1,0:T(8,128)}) %reduce-scatter.17.cloned.1.call-update) | async-done | bytes 1048592 | tf_op jit(solution)/shard_map/reduce_scatter | solution.py:249
  789.7 3.2 fusion.178
  795.8 44.0 %all-reduce.4 = (f32[1024]{0:T(1024)}, f32[1024]{0:T(1024)}, f32[1024]{0:T(1024)}, f32[1024]{0:T(1024)}, f32[1024]{0:T(1024)S(1)}) all-reduce(f32[1024]{0:T(1024)S(1)} %add.403, f32[1024]{0:T(1024)S(1)} %add.404, f32[1024]{0:T(1024)S(1)} %add.405, f32[1024]{0:T(1024)S(1)} %add.406, ...), channel_id=1, replica_groups=mesh['dp'=8,'tensor'=4] {'dp','tensor'}, use_global_device_ids=true, to_apply=%region_42.43 | all-reduce | flops 5120 | bytes 40960 | tf_op jit(solution)/shard_map/psum | solution.py:266
  839.8 30.5 %reduce-scatter.13.cloned.1.call-done = f32[1,256,1024]{2,1,0:T(8,128)} async-done(((f32[1,1024,1024]{2,1,0:T(8,128)}), f32[1,256,1024]{2,1,0:T(8,128)}) %reduce-scatter.13.cloned.1.call-update) | async-done | bytes 1048592 | tf_op jit(solution)/shard_map/reduce_scatter | solution.py:159
  870.2 79.4 %reduce-scatter.11.cloned.1.call-done = f32[1,256,1024]{2,1,0:T(8,128)} async-done(((f32[1,1024,1024]{2,1,0:T(8,128)}), f32[1,256,1024]{2,1,0:T(8,128)}) %reduce-scatter.11.cloned.1.call-update) | async-done | bytes 1048592 | tf_op jit(solution)/shard_map/reduce_scatter | solution.py:159
  954.9 45.7 %reduce-scatter.23.cloned.1.call-done = f32[128,768]{1,0:T(8,128)} async-done(((f32[1024,768]{1,0:T(8,128)}), f32[128,768]{1,0:T(8,128)}) %reduce-scatter.23.cloned.1.call-update) | async-done | bytes 393232 | tf_op jit(solution)/shard_map/reduce_scatter | solution.py:260
  1000.6 55.3 %reduce-scatter.27.cloned.1.call-done = f32[128,1024]{1,0:T(8,128)} async-done(((f32[1024,1024]{1,0:T(8,128)}), f32[128,1024]{1,0:T(8,128)}) %reduce-scatter.27.cloned.1.call-update) | async-done | bytes 524304 | tf_op jit(solution)/shard_map/reduce_scatter | solution.py:262
  (431 shorter events, 120.5 us)
Async XLA Ops:
  7.2 32.6 %all-gather.12.cloned.1.call-start = ((), (), s32[]{:S(2)}) async-start(), calls=%async_computation.11 | async-start | bytes 1769472 | tf_op jit(solution)/shard_map/all_gather | solution.py:101
  7.9 79.9 %all-gather.10.cloned.1.call-start = ((), (), s32[]{:S(2)}) async-start(), calls=%async_computation.10 | async-start | bytes 2621440 | tf_op jit(solution)/shard_map/all_gather | solution.py:97
  11.7 11.8 %copy-start.89 = (s32[2,1024]{1,0:T(2,128)S(1)}, s32[2,1024]{1,0:T(2,128)}, u32[]{:S(2)}) copy-start(s32[2,1024]{1,0:T(2,128)} %param.43) | copy-start | bytes 24580
  11.7 12.8 %copy-start.88 = (bf16[128,256]{1,0:T(8,128)(2,1)S(1)}, bf16[128,256]{1,0:T(8,128)(2,1)}, u32[]{:S(2)}) copy-start(bf16[128,256]{1,0:T(8,128)(2,1)} %param.50) | copy-start | bytes 196612
  14.8 73.0 %copy-start.113 = (f32[768]{0:T(1024)S(1)}, f32[768]{0:T(1024)}, u32[]{:S(2)}) copy-start(f32[768]{0:T(1024)} %param.49) | copy-start | bytes 9220
  14.9 119.2 %all-gather.20.cloned.1.call-start = ((), (), s32[]{:S(2)}) async-start(), calls=%async_computation.16 | async-start | bytes 2621440 | tf_op jit(solution)/shard_map/all_gather | solution.py:97
  15.6 164.6 %all-gather.24.cloned.1.call-start = ((), (), s32[]{:S(2)}) async-start(), calls=%async_computation.19 | async-start | bytes 2621440 | tf_op jit(solution)/shard_map/all_gather | solution.py:162
  16.8 209.5 %all-gather.26.cloned.1.call-start = ((), (), s32[]{:S(2)}) async-start(), calls=%async_computation.22 | async-start | bytes 2621440 | tf_op jit(solution)/shard_map/all_gather | solution.py:162
  17.4 255.6 %all-gather.22.cloned.1.call-start = ((), (), s32[]{:S(2)}) async-start(), calls=%async_computation.17 | async-start | bytes 2621440 | tf_op jit(solution)/shard_map/all_gather | solution.py:98
  18.0 283.6 %all-gather.16.cloned.1.call-start = ((), (), s32[]{:S(2)}) async-start(), calls=%async_computation.13 | async-start | bytes 2359296 | tf_op jit(solution)/shard_map/all_gather | solution.py:103
  18.7 330.9 %all-gather.14.cloned.1.call-start = ((), (), s32[]{:S(2)}) async-start(), calls=%async_computation.12 | async-start | bytes 2621440 | tf_op jit(solution)/shard_map/all_gather | solution.py:98
  19.5 410.0 %all-gather.18.cloned.1.call-start = ((), (), s32[]{:S(2)}) async-start(), calls=%async_computation.14 | async-start | bytes 2359296 | tf_op jit(solution)/shard_map/all_gather | solution.py:104
  20.2 487.9 %reduce-scatter.25.cloned.1.call-start = ((), (), s32[]{:S(2)}) async-start(), calls=%async_computation.26 | async-start | bytes 1179648 | tf_op jit(solution)/shard_map/reduce_scatter | solution.py:261
  37.2 189.1 %copy-start.21 = (bf16[1024,256]{1,0:T(8,128)(2,1)}, bf16[1024,256]{1,0:T(8,128)(2,1)S(1)}, u32[]{:S(2)}) copy-start(bf16[1024,256]{1,0:T(8,128)(2,1)S(1)} %all_gather.44) | copy-start | bytes 1572868
  37.6 173.3 %copy-start.7 = (pred[512,1024]{1,0:T(8,128)(4,1)}, pred[512,1024]{1,0:T(8,128)(4,1)S(1)}, u32[]{:S(2)}) copy-start(pred[512,1024]{1,0:T(8,128)(4,1)S(1)} %compare_and_fusion) | copy-start | bytes 1572868
  38.0 202.7 %copy-start.10 = (pred[512,1024]{1,0:T(8,128)(4,1)}, pred[512,1024]{1,0:T(8,128)(4,1)S(1)}, u32[]{:S(2)}) copy-start(pred[512,1024]{1,0:T(8,128)(4,1)S(1)} %compare_and_fusion.1) | copy-start | bytes 1572868
  38.6 148.7 %copy-start.5 = (pred[512,768]{1,0:T(8,128)(4,1)}, pred[512,768]{1,0:T(8,128)(4,1)S(1)}, u32[]{:S(2)}) copy-start(pred[512,768]{1,0:T(8,128)(4,1)S(1)} %get-tuple-element.314) | copy-start | bytes 1179652
  143.6 49.2 %copy-start.60 = (bf16[1,1024,4,16]{1,3,2,0:T(8,128)(2,1)}, bf16[1,1024,4,16]{1,3,2,0:T(8,128)(2,1)S(1)}, u32[]{:S(2)}) copy-start(bf16[1,1024,4,16]{1,3,2,0:T(8,128)(2,1)S(1)} %get-tuple-element.271) | copy-start | bytes 393220
  143.6 63.4 %copy-start.58 = (bf16[1,1024,4,16]{1,3,2,0:T(8,128)(2,1)}, bf16[1,1024,4,16]{1,3,2,0:T(8,128)(2,1)S(1)}, u32[]{:S(2)}) copy-start(bf16[1,1024,4,16]{1,3,2,0:T(8,128)(2,1)S(1)} %get-tuple-element.273) | copy-start | bytes 393220
  147.8 39.6 %copy-start.80 = (f32[4,512]{1,0:T(4,128)}, f32[4,512]{1,0:T(4,128)S(1)}, u32[]{:S(2)}) copy-start(f32[4,512]{1,0:T(4,128)S(1)} %log_add_fusion.3) | copy-start | bytes 24580
  215.9 17.9 %copy-start.23 = (bf16[1,4,1024,64]{2,3,1,0:T(8,128)(2,1)}, bf16[1,4,1024,64]{2,3,1,0:T(8,128)(2,1)S(1)}, u32[]{:S(2)}) copy-start(bf16[1,4,1024,64]{2,3,1,0:T(8,128)(2,1)S(1)} %maximum_convert_fusion.2) | copy-start | bytes 1572868
  215.9 17.9 %copy-start.25 = (bf16[1,4,1024,64]{2,3,1,0:T(8,128)(2,1)}, bf16[1,4,1024,64]{2,3,1,0:T(8,128)(2,1)S(1)}, u32[]{:S(2)}) copy-start(bf16[1,4,1024,64]{2,3,1,0:T(8,128)(2,1)S(1)} %maximum_convert_fusion.3) | copy-start | bytes 1572868
  251.6 258.2 %reduce-scatter.29.cloned.1.call-start = ((), (), s32[]{:S(2)}) async-start(), calls=%async_computation.28 | async-start | bytes 4718592 | tf_op jit(solution)/shard_map/reduce_scatter | solution.py:263
  349.6 23.9 %copy-start.41 = (bf16[1,1024,1024]{2,1,0:T(8,128)(2,1)S(1)}, bf16[1,1024,1024]{2,1,0:T(8,128)(2,1)}, u32[]{:S(2)}) copy-start(bf16[1,1024,1024]{2,1,0:T(8,128)(2,1)} %all-gather.26.cloned.1.call-done) | copy-start | bytes 6291460
  381.2 169.8 %reduce-scatter.15.cloned.1.call-start = ((), (), s32[]{:S(2)}) async-start(), calls=%async_computation.20 | async-start | bytes 5242880 | tf_op jit(solution)/shard_map/reduce_scatter | solution.py:248
  385.4 9.6 slice-start.6
  413.1 217.5 %reduce-scatter.19.cloned.1.call-start = ((), (), s32[]{:S(2)}) async-start(), calls=%async_computation.23 | async-start | bytes 5242880 | tf_op jit(solution)/shard_map/reduce_scatter | solution.py:248
  429.4 280.8 %reduce-scatter.21.cloned.1.call-start = ((), (), s32[]{:S(2)}) async-start(), calls=%async_computation.24 | async-start | bytes 5242880 | tf_op jit(solution)/shard_map/reduce_scatter | solution.py:249
  431.1 8.7 copy-start.109
  444.3 345.3 %reduce-scatter.17.cloned.1.call-start = ((), (), s32[]{:S(2)}) async-start(), calls=%async_computation.21 | async-start | bytes 5242880 | tf_op jit(solution)/shard_map/reduce_scatter | solution.py:249
  458.7 411.6 %reduce-scatter.13.cloned.1.call-start = ((), (), s32[]{:S(2)}) async-start(), calls=%async_computation.18 | async-start | bytes 5242880 | tf_op jit(solution)/shard_map/reduce_scatter | solution.py:159
  467.0 482.6 %reduce-scatter.11.cloned.1.call-start = ((), (), s32[]{:S(2)}) async-start(), calls=%async_computation.15 | async-start | bytes 5242880 | tf_op jit(solution)/shard_map/reduce_scatter | solution.py:159
  473.9 526.7 %reduce-scatter.23.cloned.1.call-start = ((), (), s32[]{:S(2)}) async-start(), calls=%async_computation.25 | async-start | bytes 3538944 | tf_op jit(solution)/shard_map/reduce_scatter | solution.py:260
  482.5 573.3 %reduce-scatter.27.cloned.1.call-start = ((), (), s32[]{:S(2)}) async-start(), calls=%async_computation.27 | async-start | bytes 4718592 | tf_op jit(solution)/shard_map/reduce_scatter | solution.py:262
  492.0 138.7 %copy-start.4 = (bf16[2,256,1024]{2,1,0:T(8,128)(2,1)S(1)}, bf16[2,256,1024]{2,1,0:T(8,128)(2,1)}, u32[]{:S(2)}) copy-start(bf16[2,256,1024]{2,1,0:T(8,128)(2,1)} %param.40) | copy-start | bytes 3145732
  492.0 138.7 %copy-start.83 = (f32[1024]{0:T(1024)S(1)}, f32[1024]{0:T(1024)}, u32[]{:S(2)}) copy-start(f32[1024]{0:T(1024)} %param.44) | copy-start | bytes 12292
  492.0 138.7 %copy-start.91 = (f32[256]{0:T(256)S(1)}, f32[256]{0:T(256)}, u32[]{:S(2)}) copy-start(f32[256]{0:T(256)} %copy-done.90) | copy-start | bytes 3076
  492.0 138.7 %copy-start.93 = (f32[256]{0:T(256)S(1)}, f32[256]{0:T(256)}, u32[]{:S(2)}) copy-start(f32[256]{0:T(256)} %copy-done.92) | copy-start | bytes 3076
  492.0 140.7 %copy-start.101 = (f32[256]{0:T(256)S(1)}, f32[256]{0:T(256)}, u32[]{:S(2)}) copy-start(f32[256]{0:T(256)} %copy-done.100) | copy-start | bytes 3076
  492.0 140.7 %copy-start.99 = (f32[256]{0:T(256)S(1)}, f32[256]{0:T(256)}, u32[]{:S(2)}) copy-start(f32[256]{0:T(256)} %copy-done.98) | copy-start | bytes 3076
  492.0 297.6 %copy-start.82 = (f32[1024]{0:T(1024)S(1)}, f32[1024]{0:T(1024)}, u32[]{:S(2)}) copy-start(f32[1024]{0:T(1024)} %param.46) | copy-start | bytes 12292
  492.0 297.6 %copy-start.95 = (f32[256]{0:T(256)S(1)}, f32[256]{0:T(256)}, u32[]{:S(2)}) copy-start(f32[256]{0:T(256)} %copy-done.94) | copy-start | bytes 3076
  492.0 297.6 %copy-start.97 = (f32[256]{0:T(256)S(1)}, f32[256]{0:T(256)}, u32[]{:S(2)}) copy-start(f32[256]{0:T(256)} %copy-done.96) | copy-start | bytes 3076
  710.2 82.8 %copy-start.14 = (f32[1,256,1024]{2,1,0:T(8,128)S(1)}, f32[1,256,1024]{2,1,0:T(8,128)}, u32[]{:S(2)}) copy-start(f32[1,256,1024]{2,1,0:T(8,128)} %reduce-scatter.21.cloned.1.call-done) | copy-start | bytes 3145732
  792.9 156.7 %copy-start.13 = (f32[1,256,1024]{2,1,0:T(8,128)S(1)}, f32[1,256,1024]{2,1,0:T(8,128)}, u32[]{:S(2)}) copy-start(f32[1,256,1024]{2,1,0:T(8,128)} %reduce-scatter.19.cloned.1.call-done) | copy-start | bytes 3145732
  792.9 156.7 %copy-start.102 = (f32[1024]{0:T(1024)S(1)}, f32[1024]{0:T(1024)}, u32[]{:S(2)}) copy-start(f32[1024]{0:T(1024)} %param.55) | copy-start | bytes 12292
  792.9 156.7 %copy-start.103 = (f32[1024]{0:T(1024)S(1)}, f32[1024]{0:T(1024)}, u32[]{:S(2)}) copy-start(f32[1024]{0:T(1024)} %param.51) | copy-start | bytes 12292
  839.7 216.1 %copy-start.104 = (f32[1024]{0:T(1024)}, f32[1024]{0:T(1024)S(1)}, u32[]{:S(2)}) copy-start(f32[1024]{0:T(1024)S(1)} %get-tuple-element.342) | copy-start | bytes 12292
  (103 other events, 344.4 us)
Sparse Core Ops, SparseCore 0:
  9.9 29.7 all-gather.11
  41.9 45.9 all-gather.9
  89.4 44.6 all-gather.19
  135.5 44.6 all-gather.23
  181.6 44.6 all-gather.25
  228.3 44.6 all-gather.21
  274.9 26.5 all-gather.15
  303.7 45.9 all-gather.13
  351.5 26.6 all-gather.17
  381.2 36.0 reduce-scatter.24
  420.7 51.3 reduce-scatter.28
  474.3 76.7 reduce-scatter.14
  553.4 77.2 reduce-scatter.18
  632.9 77.2 reduce-scatter.20
  712.3 77.2 reduce-scatter.16
  791.9 78.3 reduce-scatter.12
  872.4 77.2 reduce-scatter.10
  953.8 46.7 reduce-scatter.22
  1004.5 51.2 reduce-scatter.26
where the time goes:
time: 1070 us; the launch traced here: 1060 us
  waiting for transfers between devices  709 us (66%)
  matrix products  181 us (17%)
  blocking collectives  72.7 us (7%)
  other arithmetic  48.3 us (5%)
  local copies, waits for them, and re-layouts  35.3 us (3%)
  between operations  16.4 us (2%)
    reduce_scatter x2, waiting for transfers between devices, on_device(): lax.psum_scatter(grad_two, 'tensor', scatter_dimension=1, tiled=True)  157 us
    reduce_scatter x2, waiting for transfers between devices, on_device(): lax.psum_scatter(grad_one, 'tensor', scatter_dimension=1, tiled=True)  119 us
    reduce_scatter x2, waiting for transfers between devices, on_device(): lax.psum_scatter(partial_sum, 'tensor', scatter_dimension=1, tiled=True)  110 us
    all_gather x2, waiting for transfers between devices, on_device(): lax.all_gather(value_one.astype(jnp.bfloat16), 'tensor', axis=1, tiled=True)  85.3 us
    all_gather x2, waiting for transfers between devices, on_device(): lax.all_gather(value_two.astype(jnp.bfloat16), 'tensor', axis=1, tiled=True)  62.8 us
    reduce_scatter x1, waiting for transfers between devices, on_device(): lax.psum_scatter(grad_upw, 'dp', scatter_dimension=0, tiled=True)  55.3 us
    reduce_scatter x1, waiting for transfers between devices, on_device(): lax.psum_scatter(grad_qkv, 'dp', scatter_dimension=0, tiled=True)  45.7 us
    psum x1, blocking collectives, on_device(): lax.psum((sum_gain_one, sum_bias_one, sum_gain_two, sum_bias_two, sum_slo...  44 us
  transfers between devices with their start and end apart: 19, of which 16 were waited for; matrix products, arithmetic and copies ran while one was open for 23% of the time, Pallas kernels for 0%

commit v1 on v0

--- a/solution.py
+++ b/solution.py
@@ -159,7 +159,16 @@
         reduced = lax.psum_scatter(partial_sum, "tensor", scatter_dimension=1, tiled=True)
         out_rows.append((residual + reduced + b_out + b_down).astype(jnp.bfloat16))
         slope_local = cotangent[first_seq:last_seq]
-        slope = lax.all_gather(slope_local, "tensor", axis=1, tiled=True)
+        ring = [slope_local]
+        for hop in range(3):
+            ring.append(
+                lax.ppermute(ring[-1], "tensor", [(dev, (dev + 1) % 4) for dev in range(4)])
+            )
+        slope = jnp.roll(
+            jnp.concatenate(ring[::-1], axis=1),
+            (lax.axis_index("tensor") + 1) * ring[0].shape[1],
+            axis=1,
+        )
         qkv_full, out_full, up_full, down_full = (
             lax.all_gather(w_qkv, "dp", axis=0, tiled=True),
             lax.all_gather(w_out, "dp", axis=0, tiled=True),

time: 1070 us -> 1010 us (0.944)
  waiting for transfers between devices: 709 us -> 607 us
  other arithmetic: 48.3 us -> 80 us
  starting transfers between devices: 1.4 us -> 21.9 us
    reduce_scatter x2, waiting for transfers between devices: 119 us -> 26.8 us  [on_device(): lax.psum_scatter(grad_one, 'tensor', scatter_dimension=1, tiled=True)]
    all_gather x2, waiting for transfers between devices: 85.3 us -> 20.4 us  [on_device(): lax.all_gather(value_one.astype(jnp.bfloat16), 'tensor', axis=1, tiled=True)]
    ppermute x0 -> x6, waiting for transfers between devices: none -> 62 us  [on_device(): lax.ppermute(ring[-1], 'tensor', [(dev, (dev + 1) % 4) for dev in range(4)])]
    reduce_scatter x1, waiting for transfers between devices: 0.01 us -> 55.1 us  [on_device(): lax.psum_scatter(grad_downw, 'dp', scatter_dimension=0, tiled=True)]
    all_gather x2, waiting for transfers between devices: 62.8 us -> 9.45 us  [on_device(): lax.all_gather(value_two.astype(jnp.bfloat16), 'tensor', axis=1, tiled=True)]
    all_gather x2 -> x0, waiting for transfers between devices: 40 us -> none  [on_device(): slope = lax.all_gather(slope_local, 'tensor', axis=1, tiled=True)]
    reduce_scatter x1, waiting for transfers between devices: 0.01 us -> 34.9 us  [on_device(): lax.psum_scatter(grad_outw, 'dp', scatter_dimension=0, tiled=True)]
    all_gather x1, waiting for transfers between devices: 28.5 us -> 0.02 us  [on_device(): lax.all_gather(w_up, 'dp', axis=0, tiled=True)]
  transfers between devices with their start and end apart: 19 -> 23, of which waited for: 16 -> 17; matrix products, arithmetic and copies ran while one was open for 23% -> 27% of each run, Pallas kernels for 0% -> 0%
where the time goes in v1:
time: 1010 us; the launch traced here: 1000 us
  waiting for transfers between devices  607 us (60%)
  matrix products  183 us (18%)
  other arithmetic  80 us (8%)
  blocking collectives  69.7 us (7%)
  local copies, waits for them, and re-layouts  26.5 us (3%)
  starting transfers between devices  21.9 us (2%)
  between operations  16.4 us (2%)
    reduce_scatter x2, waiting for transfers between devices, on_device(): lax.psum_scatter(grad_two, 'tensor', scatter_dimension=1, tiled=True)  157 us
    reduce_scatter x2, waiting for transfers between devices, on_device(): lax.psum_scatter(partial_sum, 'tensor', scatter_dimension=1, tiled=True)  110 us
    ppermute x6, waiting for transfers between devices, on_device(): lax.ppermute(ring[-1], 'tensor', [(dev, (dev + 1) % 4) for dev in range(4)])  62 us
    reduce_scatter x1, waiting for transfers between devices, on_device(): lax.psum_scatter(grad_upw, 'dp', scatter_dimension=0, tiled=True)  55.5 us
    reduce_scatter x1, waiting for transfers between devices, on_device(): lax.psum_scatter(grad_downw, 'dp', scatter_dimension=0, tiled=True)  55.1 us
    reduce_scatter x1, waiting for transfers between devices, on_device(): lax.psum_scatter(grad_qkv, 'dp', scatter_dimension=0, tiled=True)  50.1 us
    psum x1, blocking collectives, on_device(): lax.psum((sum_gain_one, sum_bias_one, sum_gain_two, sum_bias_two, sum_slo...  43.8 us
    reduce_scatter x1, waiting for transfers between devices, on_device(): lax.psum_scatter(grad_outw, 'dp', scatter_dimension=0, tiled=True)  34.9 us
  transfers between devices with their start and end apart: 23, of which 17 were waited for; matrix products, arithmetic and copies ran while one was open for 27% of the time, Pallas kernels for 0%

profile of v1, /device:TPU:0, one launch (start us, length us, event | category | flops | bytes accessed | tf_op | source)
XLA Modules:
  0.0 1004.7 jit_solution(11192283898111539397)
XLA Ops:
  24.1 10.9 %all_gather.18 = bf16[1024,256]{1,0:T(8,128)(2,1)S(1)} all-gather(bf16[128,256]{1,0:T(8,128)(2,1)S(1)} %copy-done.91), channel_id=1, replica_groups=mesh['dp'=8,'tensor'=4] {'dp'}, dimensions={0}, use_global_device_ids=true | all-gather | bytes 589824 | tf_op jit(solution)/shard_map/all_gather | solution.py:102
  38.9 7.7 collective-permute-done.3
  46.7 16.1 %collective-permute-done.1 = bf16[1,256,1024]{2,1,0:T(8,128)(2,1)} collective-permute-done((bf16[1,256,1024]{2,1,0:T(8,128)(2,1)S(1)}, bf16[1,256,1024]{2,1,0:T(8,128)(2,1)}, u32[]{:S(2)}, u32[]{:S(2)}) %collective-permute-start.1) | collective-permute-done | bytes 524320 | tf_op jit(solution)/shard_map/ppermute | solution.py:165
  62.8 4.4 collective-permute-start.2
  68.9 16.3 %collective-permute-done.4 = bf16[1,256,1024]{2,1,0:T(8,128)(2,1)} collective-permute-done((bf16[1,256,1024]{2,1,0:T(8,128)(2,1)}, bf16[1,256,1024]{2,1,0:T(8,128)(2,1)}, u32[]{:S(2)}, u32[]{:S(2)}) %collective-permute-start.4) | collective-permute-done | bytes 524320 | tf_op jit(solution)/shard_map/ppermute | solution.py:165
  85.3 9.6 collective-permute-start.5
  94.9 12.8 %collective-permute-done.2 = bf16[1,256,1024]{2,1,0:T(8,128)(2,1)} collective-permute-done((bf16[1,256,1024]{2,1,0:T(8,128)(2,1)}, bf16[1,256,1024]{2,1,0:T(8,128)(2,1)}, u32[]{:S(2)}, u32[]{:S(2)}) %collective-permute-start.2) | collective-permute-done | bytes 524320 | tf_op jit(solution)/shard_map/ppermute | solution.py:165
  107.7 6.1 fusion.56
  115.5 9.0 collective-permute-done.5
  124.4 9.7 fusion.48
  146.1 20.4 %all-gather.18.cloned.1.call-done = bf16[1,1024,1024]{2,1,0:T(8,128)(2,1)} async-done(((bf16[1,256,1024]{2,1,0:T(8,128)(2,1)}), bf16[1,1024,1024]{2,1,0:T(8,128)(2,1)}) %all-gather.18.cloned.1.call-update) | async-done | bytes 2097168 | tf_op jit(solution)/shard_map/all_gather | solution.py:97
  191.3 4.7 multiply_reduce_fusion.1
  207.2 4.2 multiply_reduce_fusion.2
  211.4 4.0 multiply_convert_fusion.2
  223.0 7.2 multiply_reduce_fusion
  230.3 6.4 multiply_convert_fusion
  257.6 4.5 fusion.133
  262.1 5.2 fusion.121
  273.5 6.7 fusion.62
  280.1 9.4 all-gather.12.cloned.1.call-done
  289.6 6.5 fusion.70
  296.1 22.0 %all-gather.16.cloned.1.call-done = bf16[1024,1024]{1,0:T(8,128)(2,1)} async-done(((bf16[128,1024]{1,0:T(8,128)(2,1)}), bf16[1024,1024]{1,0:T(8,128)(2,1)}) %all-gather.16.cloned.1.call-update) | async-done | bytes 2097168 | tf_op jit(solution)/shard_map/all_gather | solution.py:104
  318.1 4.1 fusion.235
  323.4 24.4 %convert_reduce_fusion.1 = (f32[1024]{0:T(1024)S(1)}, bf16[1024,1024]{1,0:T(8,128)(2,1)}, f32[1024,1024]{1,0:T(8,128)}, f32[1024]{0:T(1024)S(1)}, bf16[1024,1024]{1,0:T(8,128)(2,1)S(1)}, /*index=5*/f32[1024,1024]{1,0:T(8,128)}) fusion(f32[1024,1024]{1,0:T(8,128)S(1)} %copy-done.41, f32[1024]{0:T(1024)S(1)} %copy-done.118, f32[1024,1024]{1,0:T(8,128)S(1)} %fusion.235, ...), kind=kOutput, calls=%fused_computation.53 | convolution fusion | flops 2304768000 | bytes 29372416 | tf_op jit(solution)/shard_map/bsd,df->bsf/dot_general | solution.py:188
  349.1 4.3 convolution_bitcast_fusion.2
  353.7 6.0 convolution_bitcast_fusion.3
  360.8 4.6 fusion.143
  365.5 5.2 fusion.137
  370.8 8.3 multiply_convert_fusion.5
  379.1 4.8 fusion.233
  387.8 4.6 fusion.142
  392.4 5.1 fusion.136
  408.0 4.0 fusion.64
  416.0 4.8 fusion.60
  420.8 4.5 fusion.76
  425.4 4.2 fusion.237
  429.7 4.6 convolution_add_fusion
  435.1 15.0 %all-reduce.5 = (f32[768]{0:T(1024)}, f32[1024]{0:T(1024)}) all-reduce(f32[768]{0:T(1024)S(1)} %add.406, f32[1024]{0:T(1024)S(1)} %add.407), channel_id=1, replica_groups=mesh['dp'=8,'tensor'=4] {'dp'}, use_global_device_ids=true, to_apply=%region_36.38 | all-reduce | flops 1792 | bytes 14336 | tf_op jit(solution)/shard_map/psum | solution.py:274
  450.1 26.8 %reduce-scatter.19.cloned.1.call-done = f32[1,256,1024]{2,1,0:T(8,128)} async-done(((f32[1,1024,1024]{2,1,0:T(8,128)}), f32[1,256,1024]{2,1,0:T(8,128)}) %reduce-scatter.19.cloned.1.call-update) | async-done | bytes 1048592 | tf_op jit(solution)/shard_map/reduce_scatter | solution.py:257
  479.0 77.3 %reduce-scatter.21.cloned.1.call-done = f32[1,256,1024]{2,1,0:T(8,128)} async-done(((f32[1,1024,1024]{2,1,0:T(8,128)}), f32[1,256,1024]{2,1,0:T(8,128)}) %reduce-scatter.21.cloned.1.call-update) | async-done | bytes 1048592 | tf_op jit(solution)/shard_map/reduce_scatter | solution.py:258
  556.3 79.7 %reduce-scatter.17.cloned.1.call-done = f32[1,256,1024]{2,1,0:T(8,128)} async-done(((f32[1,1024,1024]{2,1,0:T(8,128)}), f32[1,256,1024]{2,1,0:T(8,128)}) %reduce-scatter.17.cloned.1.call-update) | async-done | bytes 1048592 | tf_op jit(solution)/shard_map/reduce_scatter | solution.py:258
  642.2 43.8 %all-reduce.4 = (f32[1024]{0:T(1024)}, f32[1024]{0:T(1024)}, f32[1024]{0:T(1024)}, f32[1024]{0:T(1024)}, f32[1024]{0:T(1024)S(1)}) all-reduce(f32[1024]{0:T(1024)S(1)} %add.408, f32[1024]{0:T(1024)S(1)} %add.409, f32[1024]{0:T(1024)S(1)} %add.410, f32[1024]{0:T(1024)S(1)} %add.411, ...), channel_id=1, replica_groups=mesh['dp'=8,'tensor'=4] {'dp','tensor'}, use_global_device_ids=true, to_apply=%region_42.44 | all-reduce | flops 5120 | bytes 40960 | tf_op jit(solution)/shard_map/psum | solution.py:275
  686.0 30.5 %reduce-scatter.11.cloned.1.call-done = f32[1,256,1024]{2,1,0:T(8,128)} async-done(((f32[1,1024,1024]{2,1,0:T(8,128)}), f32[1,256,1024]{2,1,0:T(8,128)}) %reduce-scatter.11.cloned.1.call-update) | async-done | bytes 1048592 | tf_op jit(solution)/shard_map/reduce_scatter | solution.py:159
  716.5 79.6 %reduce-scatter.13.cloned.1.call-done = f32[1,256,1024]{2,1,0:T(8,128)} async-done(((f32[1,1024,1024]{2,1,0:T(8,128)}), f32[1,256,1024]{2,1,0:T(8,128)}) %reduce-scatter.13.cloned.1.call-update) | async-done | bytes 1048592 | tf_op jit(solution)/shard_map/reduce_scatter | solution.py:159
  801.4 34.9 %reduce-scatter.25.cloned.1.call-done = f32[128,256]{1,0:T(8,128)} async-done(((f32[1024,256]{1,0:T(8,128)}), f32[128,256]{1,0:T(8,128)}) %reduce-scatter.25.cloned.1.call-update) | async-done | bytes 131088 | tf_op jit(solution)/shard_map/reduce_scatter | solution.py:270
  836.3 50.1 %reduce-scatter.23.cloned.1.call-done = f32[128,768]{1,0:T(8,128)} async-done(((f32[1024,768]{1,0:T(8,128)}), f32[128,768]{1,0:T(8,128)}) %reduce-scatter.23.cloned.1.call-update) | async-done | bytes 393232 | tf_op jit(solution)/shard_map/reduce_scatter | solution.py:269
  886.4 55.5 %reduce-scatter.27.cloned.1.call-done = f32[128,1024]{1,0:T(8,128)} async-done(((f32[1024,1024]{1,0:T(8,128)}), f32[128,1024]{1,0:T(8,128)}) %reduce-scatter.27.cloned.1.call-update) | async-done | bytes 524304 | tf_op jit(solution)/shard_map/reduce_scatter | solution.py:271
  941.9 55.1 %reduce-scatter.29.cloned.1.call-done = f32[128,1024]{1,0:T(8,128)} async-done(((f32[1024,1024]{1,0:T(8,128)}), f32[128,1024]{1,0:T(8,128)}) %reduce-scatter.29.cloned.1.call-update) | async-done | bytes 524304 | tf_op jit(solution)/shard_map/reduce_scatter | solution.py:272
  (428 shorter events, 142.2 us)
Async XLA Ops:
  7.2 129.8 %all-gather.10.cloned.1.call-start = ((), (), s32[]{:S(2)}) async-start(), calls=%async_computation.11 | async-start | bytes 1769472 | tf_op jit(solution)/shard_map/all_gather | solution.py:101
  7.9 129.1 %all-gather.8.cloned.1.call-start = ((), (), s32[]{:S(2)}) async-start(), calls=%async_computation.10 | async-start | bytes 2621440 | tf_op jit(solution)/shard_map/all_gather | solution.py:97
  14.8 151.8 %all-gather.18.cloned.1.call-start = ((), (), s32[]{:S(2)}) async-start(), calls=%async_computation.16 | async-start | bytes 2621440 | tf_op jit(solution)/shard_map/all_gather | solution.py:97
  15.5 257.9 %all-gather.20.cloned.1.call-start = ((), (), s32[]{:S(2)}) async-start(), calls=%async_computation.17 | async-start | bytes 2621440 | tf_op jit(solution)/shard_map/all_gather | solution.py:98
  16.1 257.4 %all-gather.14.cloned.1.call-start = ((), (), s32[]{:S(2)}) async-start(), calls=%async_computation.13 | async-start | bytes 2359296 | tf_op jit(solution)/shard_map/all_gather | solution.py:103
  16.7 272.9 %all-gather.12.cloned.1.call-start = ((), (), s32[]{:S(2)}) async-start(), calls=%async_computation.12 | async-start | bytes 2621440 | tf_op jit(solution)/shard_map/all_gather | solution.py:98
  17.3 300.8 %all-gather.16.cloned.1.call-start = ((), (), s32[]{:S(2)}) async-start(), calls=%async_computation.14 | async-start | bytes 2359296 | tf_op jit(solution)/shard_map/all_gather | solution.py:104
  17.4 50.9 %copy-start.50 = (bf16[1,256,1024]{2,1,0:T(8,128)(2,1)}, bf16[1,256,1024]{2,1,0:T(8,128)(2,1)S(1)}, u32[]{:S(2)}) copy-start(bf16[1,256,1024]{2,1,0:T(8,128)(2,1)S(1)} %get-tuple-element.222) | copy-start | bytes 1572868
  17.4 18.5 %collective-permute-start = (bf16[1,256,1024]{2,1,0:T(8,128)(2,1)S(1)}, bf16[1,256,1024]{2,1,0:T(8,128)(2,1)S(1)}, u32[]{:S(2)}, u32[]{:S(2)}) collective-permute-start(bf16[1,256,1024]{2,1,0:T(8,128)(2,1)S(1)} %get-tuple-element.222), channel_id=1, source_target_pairs={{0,1},{1,2},{2,3},{3,0},{4,5},{5,6},{6,7},{7,4},{8,9},{9,10},{10,1... | collective-permute-start | bytes 1572872 | tf_op jit(solution)/shard_map/ppermute | solution.py:165
  20.5 26.1 %collective-permute-start.3 = (bf16[1,256,1024]{2,1,0:T(8,128)(2,1)S(1)}, bf16[1,256,1024]{2,1,0:T(8,128)(2,1)}, u32[]{:S(2)}, u32[]{:S(2)}) collective-permute-start(bf16[1,256,1024]{2,1,0:T(8,128)(2,1)S(1)} %get-tuple-element.223), channel_id=1, source_target_pairs={{0,1},{1,2},{2,3},{3,0},{4,5},{5,6},{6,7},{7,4},{8,9},{9,10},{10,1... | collective-permute-start | bytes 1572872 | tf_op jit(solution)/shard_map/ppermute | solution.py:165
  22.1 428.0 %reduce-scatter.15.cloned.1.call-start = ((), (), s32[]{:S(2)}) async-start(), calls=%async_computation.19 | async-start | bytes 5242880 | tf_op jit(solution)/shard_map/reduce_scatter | solution.py:257
  35.1 99.1 %copy-start.34 = (bf16[1024,256]{1,0:T(8,128)(2,1)}, bf16[1024,256]{1,0:T(8,128)(2,1)S(1)}, u32[]{:S(2)}) copy-start(bf16[1024,256]{1,0:T(8,128)(2,1)S(1)} %all_gather.18) | copy-start | bytes 1572868
  36.0 32.0 %copy-start.72 = (bf16[1,256,1024]{2,1,0:T(8,128)(2,1)}, bf16[1,256,1024]{2,1,0:T(8,128)(2,1)S(1)}, u32[]{:S(2)}) copy-start(bf16[1,256,1024]{2,1,0:T(8,128)(2,1)S(1)} %collective-permute-done) | copy-start | bytes 1572868
  36.0 26.8 %collective-permute-start.1 = (bf16[1,256,1024]{2,1,0:T(8,128)(2,1)S(1)}, bf16[1,256,1024]{2,1,0:T(8,128)(2,1)}, u32[]{:S(2)}, u32[]{:S(2)}) collective-permute-start(bf16[1,256,1024]{2,1,0:T(8,128)(2,1)S(1)} %collective-permute-done), channel_id=1, source_target_pairs={{0,1},{1,2},{2,3},{3,0},{4,5},{5,6},{6,7},{7,4},{8,9},{9,10},{10,1... | collective-permute-start | bytes 1572872 | tf_op jit(solution)/shard_map/ppermute | solution.py:165
  38.9 223.2 %copy-start.17 = (pred[512,1024]{1,0:T(8,128)(4,1)}, pred[512,1024]{1,0:T(8,128)(4,1)S(1)}, u32[]{:S(2)}) copy-start(pred[512,1024]{1,0:T(8,128)(4,1)S(1)} %compare_and_fusion) | copy-start | bytes 1572868
  46.6 38.6 %collective-permute-start.4 = (bf16[1,256,1024]{2,1,0:T(8,128)(2,1)}, bf16[1,256,1024]{2,1,0:T(8,128)(2,1)}, u32[]{:S(2)}, u32[]{:S(2)}) collective-permute-start(bf16[1,256,1024]{2,1,0:T(8,128)(2,1)} %collective-permute-done.3), channel_id=1, source_target_pairs={{0,1},{1,2},{2,3},{3,0},{4,5},{5,6},{6,7},{7,4},{8,9},{9,10},{10,1... | collective-permute-start | bytes 1572872 | tf_op jit(solution)/shard_map/ppermute | solution.py:165
  62.8 44.9 %collective-permute-start.2 = (bf16[1,256,1024]{2,1,0:T(8,128)(2,1)}, bf16[1,256,1024]{2,1,0:T(8,128)(2,1)}, u32[]{:S(2)}, u32[]{:S(2)}) collective-permute-start(bf16[1,256,1024]{2,1,0:T(8,128)(2,1)} %collective-permute-done.1), channel_id=1, source_target_pairs={{0,1},{1,2},{2,3},{3,0},{4,5},{5,6},{6,7},{7,4},{8,9},{9,10},{10,1... | collective-permute-start | bytes 1572872 | tf_op jit(solution)/shard_map/ppermute | solution.py:165
  68.3 123.0 %copy-start.19 = (pred[512,1024]{1,0:T(8,128)(4,1)}, pred[512,1024]{1,0:T(8,128)(4,1)S(1)}, u32[]{:S(2)}) copy-start(pred[512,1024]{1,0:T(8,128)(4,1)S(1)} %compare_and_fusion.1) | copy-start | bytes 1572868
  68.9 188.6 %copy-start.8 = (pred[512,768]{1,0:T(8,128)(4,1)}, pred[512,768]{1,0:T(8,128)(4,1)S(1)}, u32[]{:S(2)}) copy-start(pred[512,768]{1,0:T(8,128)(4,1)S(1)} %get-tuple-element.272) | copy-start | bytes 1179652
  85.3 39.2 %collective-permute-start.5 = (bf16[1,256,1024]{2,1,0:T(8,128)(2,1)}, bf16[1,256,1024]{2,1,0:T(8,128)(2,1)S(1)}, u32[]{:S(2)}, u32[]{:S(2)}) collective-permute-start(bf16[1,256,1024]{2,1,0:T(8,128)(2,1)} %collective-permute-done.4), channel_id=1, source_target_pairs={{0,1},{1,2},{2,3},{3,0},{4,5},{5,6},{6,7},{7,4},{8,9},{9,10},{10,1... | collective-permute-start | bytes 1572872 | tf_op jit(solution)/shard_map/ppermute | solution.py:165
  177.4 68.7 %copy-start = (f32[4,512,768]{2,1,0:T(8,128)}, f32[4,512,768]{2,1,0:T(8,128)S(1)}, u32[]{:S(2)}) copy-start(f32[4,512,768]{2,1,0:T(8,128)S(1)} %get-tuple-element.255) | copy-start | bytes 18874372
  189.0 58.8 %copy-start.2 = (f32[4,512,1024]{2,1,0:T(8,128)}, f32[4,512,1024]{2,1,0:T(8,128)S(1)}, u32[]{:S(2)}) copy-start(f32[4,512,1024]{2,1,0:T(8,128)S(1)} %get-tuple-element.253) | copy-start | bytes 25165828
  256.1 220.8 %reduce-scatter.19.cloned.1.call-start = ((), (), s32[]{:S(2)}) async-start(), calls=%async_computation.21 | async-start | bytes 5242880 | tf_op jit(solution)/shard_map/reduce_scatter | solution.py:257
  273.4 282.9 %reduce-scatter.21.cloned.1.call-start = ((), (), s32[]{:S(2)}) async-start(), calls=%async_computation.22 | async-start | bytes 5242880 | tf_op jit(solution)/shard_map/reduce_scatter | solution.py:258
  280.1 38.0 %copy-start.11 = (bf16[1024,1024]{1,0:T(8,128)(2,1)S(1)}, bf16[1024,1024]{1,0:T(8,128)(2,1)}, u32[]{:S(2)}) copy-start(bf16[1024,1024]{1,0:T(8,128)(2,1)} %copy-done.10) | copy-start | bytes 6291460
  296.1 26.1 %copy-start.118 = (f32[1024]{0:T(1024)S(1)}, f32[1024]{0:T(1024)}, u32[]{:S(2)}) copy-start(f32[1024]{0:T(1024)} %param.55) | copy-start | bytes 12292
  323.4 25.8 %copy-start.124 = (bf16[1024,1024]{1,0:T(8,128)(2,1)S(1)}, bf16[1024,1024]{1,0:T(8,128)(2,1)}, u32[]{:S(2)}) copy-start(bf16[1024,1024]{1,0:T(8,128)(2,1)} %all-gather.14.cloned.1.call-done) | copy-start | bytes 6291460
  353.5 282.5 %reduce-scatter.17.cloned.1.call-start = ((), (), s32[]{:S(2)}) async-start(), calls=%async_computation.20 | async-start | bytes 5242880 | tf_op jit(solution)/shard_map/reduce_scatter | solution.py:258
  359.8 356.7 %reduce-scatter.11.cloned.1.call-start = ((), (), s32[]{:S(2)}) async-start(), calls=%async_computation.15 | async-start | bytes 5242880 | tf_op jit(solution)/shard_map/reduce_scatter | solution.py:159
  386.7 409.4 %reduce-scatter.13.cloned.1.call-start = ((), (), s32[]{:S(2)}) async-start(), calls=%async_computation.18 | async-start | bytes 5242880 | tf_op jit(solution)/shard_map/reduce_scatter | solution.py:159
  403.0 433.4 %reduce-scatter.25.cloned.1.call-start = ((), (), s32[]{:S(2)}) async-start(), calls=%async_computation.24 | async-start | bytes 1179648 | tf_op jit(solution)/shard_map/reduce_scatter | solution.py:270
  408.0 478.4 %reduce-scatter.23.cloned.1.call-start = ((), (), s32[]{:S(2)}) async-start(), calls=%async_computation.23 | async-start | bytes 3538944 | tf_op jit(solution)/shard_map/reduce_scatter | solution.py:269
  415.6 526.3 %reduce-scatter.27.cloned.1.call-start = ((), (), s32[]{:S(2)}) async-start(), calls=%async_computation.25 | async-start | bytes 4718592 | tf_op jit(solution)/shard_map/reduce_scatter | solution.py:271
  425.4 571.7 %reduce-scatter.29.cloned.1.call-start = ((), (), s32[]{:S(2)}) async-start(), calls=%async_computation.26 | async-start | bytes 4718592 | tf_op jit(solution)/shard_map/reduce_scatter | solution.py:272
  434.3 42.6 %copy-start.4 = (bf16[2,256,1024]{2,1,0:T(8,128)(2,1)S(1)}, bf16[2,256,1024]{2,1,0:T(8,128)(2,1)}, u32[]{:S(2)}) copy-start(bf16[2,256,1024]{2,1,0:T(8,128)(2,1)} %param.42) | copy-start | bytes 3145732
  434.3 42.6 %copy-start.82 = (f32[1024]{0:T(1024)S(1)}, f32[1024]{0:T(1024)}, u32[]{:S(2)}) copy-start(f32[1024]{0:T(1024)} %param.46) | copy-start | bytes 12292
  434.3 42.6 %copy-start.94 = (f32[256]{0:T(256)S(1)}, f32[256]{0:T(256)}, u32[]{:S(2)}) copy-start(f32[256]{0:T(256)} %copy-done.93) | copy-start | bytes 3076
  434.3 42.6 %copy-start.96 = (f32[256]{0:T(256)S(1)}, f32[256]{0:T(256)}, u32[]{:S(2)}) copy-start(f32[256]{0:T(256)} %copy-done.95) | copy-start | bytes 3076
  434.3 44.6 %copy-start.114 = (f32[256]{0:T(256)S(1)}, f32[256]{0:T(256)}, u32[]{:S(2)}) copy-start(f32[256]{0:T(256)} %copy-done.113) | copy-start | bytes 3076
  434.3 44.6 %copy-start.112 = (f32[256]{0:T(256)S(1)}, f32[256]{0:T(256)}, u32[]{:S(2)}) copy-start(f32[256]{0:T(256)} %copy-done.111) | copy-start | bytes 3076
  434.3 201.7 %copy-start.81 = (f32[1024]{0:T(1024)S(1)}, f32[1024]{0:T(1024)}, u32[]{:S(2)}) copy-start(f32[1024]{0:T(1024)} %param.48) | copy-start | bytes 12292
  434.3 201.7 %copy-start.106 = (f32[256]{0:T(256)S(1)}, f32[256]{0:T(256)}, u32[]{:S(2)}) copy-start(f32[256]{0:T(256)} %copy-done.105) | copy-start | bytes 3076
  434.4 201.7 %copy-start.108 = (f32[256]{0:T(256)S(1)}, f32[256]{0:T(256)}, u32[]{:S(2)}) copy-start(f32[256]{0:T(256)} %copy-done.107) | copy-start | bytes 3076
  556.3 83.1 %copy-start.24 = (f32[1,256,1024]{2,1,0:T(8,128)S(1)}, f32[1,256,1024]{2,1,0:T(8,128)}, u32[]{:S(2)}) copy-start(f32[1,256,1024]{2,1,0:T(8,128)} %reduce-scatter.21.cloned.1.call-done) | copy-start | bytes 3145732
  639.3 156.9 %copy-start.22 = (f32[1,256,1024]{2,1,0:T(8,128)S(1)}, f32[1,256,1024]{2,1,0:T(8,128)}, u32[]{:S(2)}) copy-start(f32[1,256,1024]{2,1,0:T(8,128)} %reduce-scatter.19.cloned.1.call-done) | copy-start | bytes 3145732
  639.3 156.9 %copy-start.115 = (f32[1024]{0:T(1024)S(1)}, f32[1024]{0:T(1024)}, u32[]{:S(2)}) copy-start(f32[1024]{0:T(1024)} %param.57) | copy-start | bytes 12292
  639.3 156.8 %copy-start.116 = (f32[1024]{0:T(1024)S(1)}, f32[1024]{0:T(1024)}, u32[]{:S(2)}) copy-start(f32[1024]{0:T(1024)} %param.53) | copy-start | bytes 12292
  686.0 311.0 %copy-start.117 = (f32[1024]{0:T(1024)}, f32[1024]{0:T(1024)S(1)}, u32[]{:S(2)}) copy-start(f32[1024]{0:T(1024)S(1)} %get-tuple-element.301) | copy-start | bytes 12292
  (105 other events, 432.9 us)
Sparse Core Ops, SparseCore 0:
  9.9 28.9 all-gather.9
  41.1 79.5 all-gather.7
  122.3 44.2 all-gather.17
  168.5 44.6 all-gather.19
  214.9 26.6 all-gather.13
  243.6 45.9 all-gather.11
  291.4 26.6 all-gather.15
  320.4 76.7 reduce-scatter.14
  399.6 77.2 reduce-scatter.18
  479.0 77.2 reduce-scatter.20
  558.7 77.2 reduce-scatter.16
  638.2 78.2 reduce-scatter.10
  718.9 77.1 reduce-scatter.12
  799.8 36.5 reduce-scatter.24
  840.1 46.2 reduce-scatter.22
  890.5 51.3 reduce-scatter.26
  945.7 51.3 reduce-scatter.28
